TPU v7x, 128 devices: a whole 4x4x4 slice. The times are simulated.
128 devices in a mesh: row: 8 (over z, core), col: 16 (over y, x).
Axes of the slice: x: 4, y: 4, z: 4, core: 2. Of those that a mesh axis runs over, the one named last changes fastest.
Arguments:
- tiles: bfloat16 [16384, 128, 128], P(('row', 'col')), may hold values from -6 to 6
- tile_target: int32 [16384, 1], P(('row', 'col')), may hold values from 0 to 127; in each aligned block of 128 rows (0 to 127, 128 to 255, ...) at most 2 rows name the same one
- tile_place: int32 [16384], P(('row', 'col')), may hold values from 0 to 95
- density: bfloat16 [8192, 16384], P('col', 'row'), may hold values from -0.125 to 0.125
Outputs:
- contracted: bfloat16 [49152, 16384], P('col', 'row')
Inputs may be any that keep to these rules, and one draw needn't show every extreme that they name: `tile_target`: among the tiles of one device, at most 2 name the same grid position, and some device has exactly 2 tiles for one position.
All inputs are finite; a program needn't handle non-finite values.
Results may differ from a plain program's by a relative error of at most 0.0046.
Values may be sent and summed in bfloat16 or wider, within the bound.
A program may use at most 256 MiB of HBM per device.

v0:
```python
import jax
import jax.numpy as jnp
from jax import lax
from jax.sharding import PartitionSpec as P

ROW_BLOCKS_DEV = 24
K_BLOCKS = 4
STEPS = 4
POSITIONS = 96


def passed_along(value, axis, steps):
    count = lax.axis_size(axis)
    pairs = [(source, (source + steps) % count) for source in range(count)]
    return lax.ppermute(value, axis, pairs)


def on_device(tiles, tile_target, tile_place, density):
    row_count = lax.axis_size("row")
    col_count = lax.axis_size("col")
    devices = row_count * col_count
    tile_count = tiles.shape[0]
    tile_size = tiles.shape[1]
    capacity = max(2, (2 * tile_count + devices - 1) // devices)
    slots = devices * capacity
    targets = tile_target[:, 0]
    order = jnp.arange(tile_count, dtype=jnp.int32)
    same_target = targets[:, None] == targets[None, :]
    earlier = order[None, :] < order[:, None]
    ranks = jnp.sum((same_target & earlier).astype(jnp.int32), axis=1)
    slot_of = targets * capacity + ranks
    hits = slot_of[None, :] == jnp.arange(slots, dtype=jnp.int32)[:, None]
    filled = jnp.any(hits, axis=1)
    source = jnp.sum(jnp.where(hits, order[None, :], 0), axis=1)
    padded_tiles = jnp.concatenate(
        [tiles, jnp.zeros((1, tile_size, tile_size), tiles.dtype)], axis=0
    )
    send_tiles = jnp.take(padded_tiles, jnp.where(filled, source, tile_count), axis=0)
    send_places = jnp.where(filled, jnp.take(tile_place, source), -1)
    flat_tiles = send_tiles.reshape(devices, capacity, tile_size, tile_size)
    flat_places = send_places.reshape(devices, capacity)
    got_tiles, got_places = (
        lax.all_to_all(flat_tiles, ("row", "col"), split_axis=0, concat_axis=0, tiled=True),
        lax.all_to_all(flat_places, ("row", "col"), split_axis=0, concat_axis=0, tiled=True),
    )
    got_tiles = got_tiles.reshape(slots, tile_size * tile_size)
    got_places = got_places.reshape(slots)
    selector = (got_places[None, :] == jnp.arange(POSITIONS, dtype=jnp.int32)[:, None]).astype(
        jnp.bfloat16
    )
    dense = jnp.dot(selector, got_tiles, preferred_element_type=jnp.float32)
    dense = dense.reshape(ROW_BLOCKS_DEV, K_BLOCKS, tile_size, tile_size).transpose(0, 2, 1, 3)
    panel = dense.reshape(ROW_BLOCKS_DEV * tile_size, K_BLOCKS * tile_size).astype(jnp.bfloat16)
    total = jnp.zeros((panel.shape[0], density.shape[1]), jnp.float32)
    left, right = (panel, density)
    for offset in range(STEPS):
        total = total + jnp.dot(left, right, preferred_element_type=jnp.float32)
        if offset + 1 < STEPS:
            left = passed_along(left, "row", -1)
            right = passed_along(right, "col", -1)
    return total.astype(jnp.bfloat16)


def solution(mesh):
    in_specs = (
        P(("row", "col"), None, None),
        P(("row", "col"), None),
        P(("row", "col")),
        P("col", "row"),
    )
    out_specs = P("col", "row")
    return jax.shard_map(
        on_device, mesh=mesh, in_specs=in_specs, out_specs=out_specs, check_vma=False
    )
```

profile of v0, /device:TPU:30, one launch (start us, length us, event | category | flops | bytes accessed | tf_op | source)
XLA Modules:
  0.0 377.5 jit_solution(2991988348471266212)
XLA Ops:
  0.0 0.0 copy-start
  0.0 0.9 convert_reduce_fusion
  0.9 0.7 multiply_add_fusion.1
  1.6 0.1 fusion
  1.7 0.1 select_reduce_fusion
  1.8 0.2 reduce_or.14
  2.0 0.1 reduce_sum.24
  2.1 0.0 copy-done
  2.2 1.9 gather_fusion
  4.0 0.1 gather.13
  4.2 0.6 select_select_fusion
  4.8 10.2 %all-to-all-start = ((s32[128,1,2]{2,1,0:T(1,128)}), s32[128,1,2]{2,1,0:T(1,128)S(1)}, u32[]{:S(2)}, u32[]{:S(2)}) async-start(s32[128,1,2]{2,1,0:T(1,128)} %bitcast.3), calls=%async_computation | async-start | bytes 131072 | tf_op jit(solution)/shard_map/all_to_all | solution.py:44
  15.1 0.1 select_n.97
  15.3 5.7 %concatenate.3 = bf16[129,128,128]{2,1,0:T(8,128)(2,1)} pad(bf16[128,128,128]{2,1,0:T(8,128)(2,1)} %param.4, bf16[]{:T(256)} %constant.40.clone.1), padding=0_1x0_0x0_0 | pad | bytes 8421378 | tf_op jit(solution)/shard_map/concatenate | solution.py:35
  21.0 10.8 %gather_fusion.1 = bf16[256,128,128]{2,1,0:T(8,128)(2,1)} fusion(bf16[129,128,128]{2,1,0:T(8,128)(2,1)} %concatenate.3, s32[1024]{0:T(1024)S(1)} %pad_clamp_fusion), kind=kCustom, calls=%fused_computation.1 | custom fusion | bytes 16778240 | tf_op jit(solution)/shard_map/jit(_take)/gather | solution.py:38
  31.8 7.6 %broadcast_select_fusion = bf16[128,2,128,128]{3,2,1,0:T(8,128)(2,1)} fusion(bf16[128,2,128,128]{3,2,1,0:T(8,128)(2,1)} %bitcast.41, pred[128,2]{1,0:T(8,128)(4,1)S(1)} %compare_and_fusion), kind=kLoop, calls=%fused_computation.4 | loop fusion | flops 4194304 | bytes 16777472 | tf_op jit(solution)/shard_map/jit(_take)/select_n | solution.py:38
  39.4 0.0 all-to-all-done
  39.4 10.7 %all-to-all-start.1 = ((bf16[128,2,128,128]{3,2,1,0:T(8,128)(2,1)}), bf16[128,2,128,128]{3,2,1,0:T(8,128)(2,1)}, u32[]{:S(2)}, u32[]{:S(2)}) async-start(bf16[128,2,128,128]{3,2,1,0:T(8,128)(2,1)} %broadcast_select_fusion), calls=%async_computation.1 | async-start | bytes 16777216 | tf_op jit(solution)/shard_map/all_to_all | solution.py:43
  50.1 0.5 broadcast.149
  50.7 0.8 reduce.3
  51.4 0.1 eq.58
  51.6 95.7 %all-to-all-done.1 = bf16[128,2,128,128]{3,2,1,0:T(8,128)(2,1)} async-done(((bf16[128,2,128,128]{3,2,1,0:T(8,128)(2,1)}), bf16[128,2,128,128]{3,2,1,0:T(8,128)(2,1)}, u32[]{:S(2)}, u32[]{:S(2)}) %all-to-all-start.1) | async-done | bytes 8388640 | tf_op jit(solution)/shard_map/all_to_all | solution.py:43
  147.3 23.3 %copy.20 = bf16[32,8,128,128]{3,1,2,0:T(8,128)(2,1)} copy(bf16[32,8,128,128]{3,2,1,0:T(8,128)(2,1)} %bitcast.15) | data formatting | bytes 16777216
  170.6 11.9 %copy.12 = bf16[16384,256]{1,0:T(8,128)(2,1)} copy(bf16[16384,256]{0,1:T(8,128)(2,1)} %bitcast.42) | data formatting | bytes 16777216 | tf_op jit(solution)/shard_map/dot_general | solution.py:51
  182.5 7.7 %convert_bitcast_fusion = bf16[24,128,4,128]{3,0,1,2:T(8,128)(2,1)} fusion(bf16[128,128,256,1]{2,1,0,3:T(8,128)(2,1)} %bitcast.45, s32[24,4]{0,1:T(4,128)S(1)} %multiply_add_fusion, s32[256]{0:T(256)S(1)} %eq.58), kind=kOutput, calls=%fused_computation.6 | convolution fusion | flops 806903808 | bytes 11535744 | tf_op jit(solution)/shard_map/dot_general | solution.py:51
  190.3 4.3 %copy.13 = bf16[24,128,4,128]{1,0,3,2:T(8,128)(2,1)S(1)} copy(bf16[24,128,4,128]{3,0,1,2:T(8,128)(2,1)} %convert_bitcast_fusion) | data formatting | bytes 6291456 | tf_op jit(solution)/shard_map/convert_element_type | solution.py:53
  194.6 0.0 copy-start.2
  194.6 0.9 copy.21
  195.5 0.0 collective-permute-start
  195.5 0.7 copy-done.2
  196.2 4.1 %collective-permute-start.1 = (bf16[512,2048]{1,0:T(8,128)(2,1)S(1)}, bf16[512,2048]{1,0:T(8,128)(2,1)S(1)}, u32[]{:S(2)}, u32[]{:S(2)}) collective-permute-start(bf16[512,2048]{1,0:T(8,128)(2,1)S(1)} %copy-done.2), channel_id=1, source_target_pairs={{0,15},{1,0},{2,1},{3,2},{4,3},{5,4},{6,5},{7,6},{8,7},{9,8},{10,9... | collective-permute-start | bytes 6291464 | tf_op jit(solution)/shard_map/ppermute | solution.py:15
  200.3 29.9 %collective-permute-done = bf16[3072,512]{0,1:T(8,128)(2,1)S(1)} collective-permute-done((bf16[3072,512]{0,1:T(8,128)(2,1)S(1)}, bf16[3072,512]{0,1:T(8,128)(2,1)S(1)}, u32[]{:S(2)}, u32[]{:S(2)}) %collective-permute-start) | collective-permute-done | bytes 3145760 | tf_op jit(solution)/shard_map/ppermute | solution.py:15
  230.3 3.4 collective-permute-start.2
  233.7 13.2 %collective-permute-done.1 = bf16[512,2048]{1,0:T(8,128)(2,1)S(1)} collective-permute-done((bf16[512,2048]{1,0:T(8,128)(2,1)S(1)}, bf16[512,2048]{1,0:T(8,128)(2,1)S(1)}, u32[]{:S(2)}, u32[]{:S(2)}) %collective-permute-start.1) | collective-permute-done | bytes 2097184 | tf_op jit(solution)/shard_map/ppermute | solution.py:15
  246.9 1.7 collective-permute-start.3
  248.6 48.2 %collective-permute-done.3 = bf16[512,2048]{1,0:T(8,128)(2,1)S(1)} collective-permute-done((bf16[512,2048]{1,0:T(8,128)(2,1)S(1)}, bf16[512,2048]{1,0:T(8,128)(2,1)S(1)}, u32[]{:S(2)}, u32[]{:S(2)}) %collective-permute-start.3) | collective-permute-done | bytes 2097184 | tf_op jit(solution)/shard_map/ppermute | solution.py:15
  296.7 0.0 collective-permute-start.5
  296.7 0.0 collective-permute-done.2
  296.7 0.0 collective-permute-start.4
  296.8 11.9 %fusion.6 = f32[3072,2048]{1,0:T(8,128)} fusion(bf16[512,2048]{1,0:T(8,128)(2,1)S(1)} %copy-done.2, bf16[64,8,24,128]{3,2,1,0:T(8,128)(2,1)S(1)} %bitcast.44), kind=kOutput, calls=%fused_computation.29 | convolution fusion | flops 6442450944 | bytes 30408704 | tf_op jit(solution)/shard_map/dot_general | solution.py:57
  308.7 11.7 %fusion.7 = f32[3072,2048]{1,0:T(8,128)} fusion(bf16[3072,512]{0,1:T(8,128)(2,1)S(1)} %collective-permute-done, bf16[512,2048]{1,0:T(8,128)(2,1)S(1)} %collective-permute-done.1), kind=kOutput, calls=%fused_computation.30 | convolution fusion | flops 6442450944 | bytes 30408704 | tf_op jit(solution)/shard_map/dot_general | solution.py:57
  320.4 11.7 %fusion.8 = f32[3072,2048]{1,0:T(8,128)} fusion(bf16[3072,512]{0,1:T(8,128)(2,1)S(1)} %collective-permute-done.2, bf16[512,2048]{1,0:T(8,128)(2,1)S(1)} %collective-permute-done.3), kind=kOutput, calls=%fused_computation.31 | convolution fusion | flops 6442450944 | bytes 30408704 | tf_op jit(solution)/shard_map/dot_general | solution.py:57
  332.1 13.8 %collective-permute-done.5 = bf16[512,2048]{1,0:T(8,128)(2,1)} collective-permute-done((bf16[512,2048]{1,0:T(8,128)(2,1)S(1)}, bf16[512,2048]{1,0:T(8,128)(2,1)}, u32[]{:S(2)}, u32[]{:S(2)}) %collective-permute-start.5) | collective-permute-done | bytes 2097184 | tf_op jit(solution)/shard_map/ppermute | solution.py:15
  345.9 0.0 collective-permute-done.4
  345.9 0.0 copy-start.1
  345.9 31.4 %add_convert_fusion = bf16[3072,2048]{1,0:T(8,128)(2,1)} fusion(f32[3072,2048]{1,0:T(8,128)} %fusion.8, f32[3072,2048]{1,0:T(8,128)} %fusion.6, f32[3072,2048]{1,0:T(8,128)} %fusion.7, bf16[3072,512]{0,1:T(8,128)(2,1)} %collective-permute-done.4, bf16[512,2048]{1,0:T(8,128)(2,1)} %collective-permute-done.5), kind=kOutput, calls=%fused_computation.2 | convolution fusion | flops 6467616768 | bytes 93323264 | tf_op jit(solution)/shard_map/dot_general | solution.py:57
  377.3 0.0 copy-done.1
  (6 shorter events, 0.1 us)
Async XLA Ops:
  0.0 2.1 copy-start
  4.8 34.6 %all-to-all-start = ((s32[128,1,2]{2,1,0:T(1,128)}), s32[128,1,2]{2,1,0:T(1,128)S(1)}, u32[]{:S(2)}, u32[]{:S(2)}) async-start(s32[128,1,2]{2,1,0:T(1,128)} %bitcast.3), calls=%async_computation | async-start | bytes 131072 | tf_op jit(solution)/shard_map/all_to_all | solution.py:44
  39.4 107.9 %all-to-all-start.1 = ((bf16[128,2,128,128]{3,2,1,0:T(8,128)(2,1)}), bf16[128,2,128,128]{3,2,1,0:T(8,128)(2,1)}, u32[]{:S(2)}, u32[]{:S(2)}) async-start(bf16[128,2,128,128]{3,2,1,0:T(8,128)(2,1)} %broadcast_select_fusion), calls=%async_computation.1 | async-start | bytes 16777216 | tf_op jit(solution)/shard_map/all_to_all | solution.py:43
  194.6 1.6 copy-start.2
  195.5 34.8 %collective-permute-start = (bf16[3072,512]{0,1:T(8,128)(2,1)S(1)}, bf16[3072,512]{0,1:T(8,128)(2,1)S(1)}, u32[]{:S(2)}, u32[]{:S(2)}) collective-permute-start(bf16[3072,512]{0,1:T(8,128)(2,1)S(1)} %bitcast.46), channel_id=1, source_target_pairs={{0,112},{16,0},{32,16},{48,32},{64,48},{80,64},{96,80},{112,96},{1... | collective-permute-start | bytes 9437192 | tf_op jit(solution)/shard_map/ppermute | solution.py:15
  196.2 50.7 %collective-permute-start.1 = (bf16[512,2048]{1,0:T(8,128)(2,1)S(1)}, bf16[512,2048]{1,0:T(8,128)(2,1)S(1)}, u32[]{:S(2)}, u32[]{:S(2)}) collective-permute-start(bf16[512,2048]{1,0:T(8,128)(2,1)S(1)} %copy-done.2), channel_id=1, source_target_pairs={{0,15},{1,0},{2,1},{3,2},{4,3},{5,4},{6,5},{7,6},{8,7},{9,8},{10,9... | collective-permute-start | bytes 6291464 | tf_op jit(solution)/shard_map/ppermute | solution.py:15
  230.3 66.5 %collective-permute-start.2 = (bf16[3072,512]{0,1:T(8,128)(2,1)S(1)}, bf16[3072,512]{0,1:T(8,128)(2,1)S(1)}, u32[]{:S(2)}, u32[]{:S(2)}) collective-permute-start(bf16[3072,512]{0,1:T(8,128)(2,1)S(1)} %collective-permute-done), channel_id=1, source_target_pairs={{0,112},{16,0},{32,16},{48,32},{64,48},{80,64},{96,80},{112,96},{1... | collective-permute-start | bytes 9437192 | tf_op jit(solution)/shard_map/ppermute | solution.py:15
  246.9 49.9 %collective-permute-start.3 = (bf16[512,2048]{1,0:T(8,128)(2,1)S(1)}, bf16[512,2048]{1,0:T(8,128)(2,1)S(1)}, u32[]{:S(2)}, u32[]{:S(2)}) collective-permute-start(bf16[512,2048]{1,0:T(8,128)(2,1)S(1)} %collective-permute-done.1), channel_id=1, source_target_pairs={{0,15},{1,0},{2,1},{3,2},{4,3},{5,4},{6,5},{7,6},{8,7},{9,8},{10,9... | collective-permute-start | bytes 6291464 | tf_op jit(solution)/shard_map/ppermute | solution.py:15
  296.7 49.1 %collective-permute-start.5 = (bf16[512,2048]{1,0:T(8,128)(2,1)S(1)}, bf16[512,2048]{1,0:T(8,128)(2,1)}, u32[]{:S(2)}, u32[]{:S(2)}) collective-permute-start(bf16[512,2048]{1,0:T(8,128)(2,1)S(1)} %collective-permute-done.3), channel_id=1, source_target_pairs={{0,15},{1,0},{2,1},{3,2},{4,3},{5,4},{6,5},{7,6},{8,7},{9,8},{10,9... | collective-permute-start | bytes 6291464 | tf_op jit(solution)/shard_map/ppermute | solution.py:15
  296.7 49.1 %collective-permute-start.4 = (bf16[3072,512]{0,1:T(8,128)(2,1)S(1)}, bf16[3072,512]{0,1:T(8,128)(2,1)}, u32[]{:S(2)}, u32[]{:S(2)}) collective-permute-start(bf16[3072,512]{0,1:T(8,128)(2,1)S(1)} %collective-permute-done.2), channel_id=1, source_target_pairs={{0,112},{16,0},{32,16},{48,32},{64,48},{80,64},{96,80},{112,96},{1... | collective-permute-start | bytes 9437192 | tf_op jit(solution)/shard_map/ppermute | solution.py:15
  345.9 31.4 %copy-start.1 = (s32[128]{0:T(128)S(1)}, s32[128]{0:T(128)}, u32[]{:S(2)}) copy-start(s32[128]{0:T(128)} %param.6) | copy-start | bytes 1540
where the time goes:
time: 383 us; the launch traced here: 378 us
  waiting for transfers between devices  201 us (52%)
  matrix products  74.5 us (19%)
  local copies, waits for them, and re-layouts  60.8 us (16%)
  starting transfers between devices  30.2 us (8%)
  other arithmetic  10.9 us (3%)
    ppermute x6, waiting for transfers between devices, passed_along(): return lax.ppermute(value, axis, pairs)  105 us
    all_to_all x1, waiting for transfers between devices, on_device(): lax.all_to_all(flat_tiles, ('row', 'col'), split_axis=0, concat_axis=0, t...  95.7 us
    dot_general x4, matrix products, on_device(): total = total + jnp.dot(left, right, preferred_element_type=jnp.float32)  66.7 us
    unnamed x8, local copies, waits for them, and re-layouts  24.9 us
    dot_general x1, local copies, waits for them, and re-layouts, on_device(): dense = jnp.dot(selector, got_tiles, preferred_element_type=jnp.float32)  11.9 us
    gather x1, local copies, waits for them, and re-layouts, on_device(): jnp.take(padded_tiles, jnp.where(filled, source, tile_count), axis=0)  10.8 us
    all_to_all x1, starting transfers between devices, on_device(): lax.all_to_all(flat_tiles, ('row', 'col'), split_axis=0, concat_axis=0, t...  10.7 us
    all_to_all x1, starting transfers between devices, on_device(): lax.all_to_all(flat_places, ('row', 'col'), split_axis=0, concat_axis=0,...  10.2 us
  transfers between devices with their start and end apart: 8, of which 5 were waited for; matrix products, arithmetic and copies ran while one was open for 16% of the time, Pallas kernels for 0%

commit v1 on v0

v1 whole, which is shorter than its diff:
```python
import functools

import jax
import jax.numpy as jnp
from jax import lax
from jax.experimental import pallas as pl
from jax.experimental.pallas import tpu as pltpu
from jax.sharding import PartitionSpec as P

K_BLOCKS = 4
POSITIONS = 96
CAP = 2
CHUNKS = 3


def permuted(value, axis, pairs):
    return lax.ppermute(value, axis, pairs)


def shifted(value, axis, steps):
    count = lax.axis_size(axis)
    return permuted(value, axis, [(s, (s + steps) % count) for s in range(count)])


def pack_kernel(shift, devices, target_ref, place_ref, tiles_ref, send_ref, places_ref, held, used, slots, in_sem, out_sem):
    tile_count = tiles_ref.shape[0]
    load = pltpu.make_async_copy(tiles_ref, held, in_sem)
    load.start()

    @pl.loop(0, devices)
    def _(d):
        used[d] = 0
        for c in range(CAP):
            places_ref[d * CAP + c] = -1

    @pl.loop(0, tile_count)
    def _(t):
        dest = lax.rem(target_ref[t] + shift, devices)
        rank = used[dest]
        used[dest] = rank + 1
        slot = dest * CAP + rank
        slots[t] = slot
        places_ref[slot] = place_ref[t]

    load.wait()

    @pl.loop(0, tile_count)
    def _(t):
        pltpu.make_async_copy(held.at[t], send_ref.at[slots[t]], out_sem).start()

    pltpu.make_async_copy(held, send_ref.at[pl.ds(0, tile_count)], out_sem).wait()


def pack(tiles, targets, places, shift, devices):
    tile_count, size, _ = tiles.shape
    smem = pl.BlockSpec(memory_space=pltpu.SMEM)
    return pl.pallas_call(
        functools.partial(pack_kernel, shift, devices),
        out_shape=(
            jax.ShapeDtypeStruct((devices * CAP, size, size), tiles.dtype),
            jax.ShapeDtypeStruct((devices * CAP,), jnp.int32),
        ),
        in_specs=[smem, smem, pl.BlockSpec(memory_space=pl.ANY)],
        out_specs=(pl.BlockSpec(memory_space=pl.ANY), smem),
        scratch_shapes=[
            pltpu.VMEM(tiles.shape, tiles.dtype),
            pltpu.SMEM((devices,), jnp.int32),
            pltpu.SMEM((tile_count,), jnp.int32),
            pltpu.SemaphoreType.DMA,
            pltpu.SemaphoreType.DMA,
        ],
        name="pack",
    )(targets, places, tiles)


def add_kernel(groups, place_ref, got_ref, panel_ref, held, total, seen, sems):
    slots, size, _ = got_ref.shape
    per = slots // groups

    def copy(g):
        part = pl.ds(g * per, per)
        return pltpu.make_async_copy(got_ref.at[part], held.at[part], sems.at[g])

    for g in range(groups):
        copy(g).start()

    @pl.loop(0, POSITIONS)
    def _(b):
        seen[b] = 0

    for g in range(groups):
        copy(g).wait()

        @pl.loop(g * per, (g + 1) * per)
        def _(s):
            place = place_ref[s]

            @pl.when(place >= 0)
            def _():
                first = seen[place] == 0
                tile = held[s].astype(jnp.float32)

                @pl.when(first)
                def _():
                    total[place] = tile
                    seen[place] = 1

                @pl.when(jnp.logical_not(first))
                def _():
                    total[place] += tile

    @pl.loop(0, POSITIONS // K_BLOCKS)
    def _(r):
        rows = pl.ds(pl.multiple_of(r * size, size), size)
        for k in range(K_BLOCKS):
            block = r * K_BLOCKS + k
            value = jnp.where(seen[block] > 0, total[block], 0.0)
            panel_ref[rows, k * size:(k + 1) * size] = value.astype(panel_ref.dtype)


def add_tiles(got, places):
    slots, size, _ = got.shape
    groups = 8
    return pl.pallas_call(
        functools.partial(add_kernel, groups),
        out_shape=jax.ShapeDtypeStruct((POSITIONS // K_BLOCKS * size, K_BLOCKS * size), got.dtype),
        in_specs=[pl.BlockSpec(memory_space=pltpu.SMEM), pl.BlockSpec(memory_space=pl.ANY)],
        out_specs=pl.BlockSpec(memory_space=pltpu.VMEM),
        scratch_shapes=[
            pltpu.VMEM(got.shape, got.dtype),
            pltpu.VMEM((POSITIONS, size, size), jnp.float32),
            pltpu.SMEM((POSITIONS,), jnp.int32),
            pltpu.SemaphoreType.DMA((groups,)),
        ],
        name="add_tiles",
    )(places, got)


def product_kernel(steps, wide, *refs):
    lefts, rights, out_ref = refs[:steps], refs[steps:2 * steps], refs[-1]
    left = jnp.concatenate([ref[...] for ref in lefts], axis=1)
    for n in range(0, out_ref.shape[1], wide):
        right = jnp.concatenate([ref[:, n:n + wide] for ref in rights], axis=0)
        out = jnp.dot(left, right, preferred_element_type=jnp.float32)
        out_ref[:, n:n + wide] = out.astype(out_ref.dtype)


def product(lefts, rights, start, rows_all, out):
    rows, depth = lefts[0].shape
    columns = rights[0].shape[1]
    tall = 256
    steps = len(lefts)
    base = start // tall
    body = functools.partial(product_kernel, steps, 512)
    args = list(lefts) + list(rights)
    specs = [pl.BlockSpec((tall, depth), lambda m: (m, 0))] * steps
    specs += [pl.BlockSpec((depth, columns), lambda m: (0, 0), pipeline_mode=pl.Buffered(1))] * steps
    aliases = {}
    if out is not None:
        args.append(out)
        specs.append(pl.BlockSpec(memory_space=pl.ANY))
        aliases = {2 * steps: 0}
    return pl.pallas_call(
        body,
        grid=(rows // tall,),
        out_shape=jax.ShapeDtypeStruct((rows_all, columns), jnp.bfloat16),
        in_specs=specs,
        out_specs=pl.BlockSpec((tall, columns), lambda m: (m + base, 0)),
        input_output_aliases=aliases,
        cost_estimate=pl.CostEstimate(
            flops=2 * rows * columns * depth * steps,
            bytes_accessed=2 * (rows * columns + steps * depth * (rows + columns)),
            transcendentals=0,
        ),
        name="product",
    )(*args)


def on_device(tiles, tile_target, tile_place, density):
    row_count = lax.axis_size("row")
    col_count = lax.axis_size("col")
    devices = row_count * col_count
    size = tiles.shape[1]
    send, places = pack(tiles, tile_target[:, 0], tile_place, devices - col_count, devices)
    got = lax.all_to_all(send.reshape(devices, CAP, size, size), ("row", "col"), split_axis=0, concat_axis=0, tiled=True)
    got_places = lax.all_to_all(places.reshape(devices, CAP), ("row", "col"), split_axis=0, concat_axis=0, tiled=True)
    one = shifted(density, "col", -1)
    three = shifted(density, "col", -3)
    half = density.shape[1] // 2
    two = jnp.concatenate([shifted(one[:, :half], "col", -1), shifted(three[:, half:], "col", 1)], axis=1)
    rights = (density, one, two, three)

    panel = add_tiles(got.reshape(devices * CAP, size, size), got_places.reshape(devices * CAP))
    even = lax.axis_index("row") % 2 == 0
    swap = [(s, s ^ 1) for s in range(row_count)]
    rows_all = panel.shape[0]
    rows = rows_all // CHUNKS
    lefts = []
    for c in range(CHUNKS):
        own = panel[c * rows:(c + 1) * rows]
        last = shifted(own, "row", -2)
        first = shifted(own, "row", 1)
        mid = permuted(jnp.where(even, last, own), "row", swap)
        lefts.append((first, own, mid, last))
    out = None
    for c in range(CHUNKS):
        out = product(lefts[c], rights, c * rows, rows_all, out)
    return out


def solution(mesh):
    in_specs = (
        P(("row", "col"), None, None),
        P(("row", "col"), None),
        P(("row", "col")),
        P("col", "row"),
    )
    return jax.shard_map(on_device, mesh=mesh, in_specs=in_specs, out_specs=P("col", "row"), check_vma=False)
```

time: 383 us -> 336 us (0.88)
  matrix products: 74.5 us -> 0 us
  Pallas kernels: 0 us -> 58.1 us
  local copies, waits for them, and re-layouts: 60.8 us -> 6.88 us
  blocking collectives: 0 us -> 16.9 us
  waiting for transfers between devices: 201 us -> 215 us
  other arithmetic: 10.9 us -> 6.14 us
    dot_general x5 -> x0, matrix products: 74.5 us -> none  [the longest x4 66.7 us: on_device(): total = total + jnp.dot(left, right, preferred_element_type=jnp.float32)]
    pallas_call x0 -> x5, Pallas kernels: none -> 58.1 us  [the longest x3 42.9 us: product(): pl.pallas_call(body, grid=(rows // tall,), out_shape=jax.ShapeDtypeStruct...]
    unnamed x8 -> x19, local copies, waits for them, and re-layouts: 24.9 us -> 2.19 us
    all_to_all x0 -> x1, blocking collectives: none -> 16.9 us  [on_device(): lax.all_to_all(places.reshape(devices, CAP), ('row', 'col'), split_axis=0...]
    ppermute x6 -> x13, waiting for transfers between devices: 105 us -> 120 us  [permuted(): return lax.ppermute(value, axis, pairs)]
    gather x3 -> x0, local copies, waits for them, and re-layouts: 12.8 us -> none  [the longest x1 10.8 us: on_device(): jnp.take(padded_tiles, jnp.where(filled, source, tile_count), axis=0)]
    all_to_all x2 -> x1, starting transfers between devices: 20.9 us -> 8.52 us  [on_device(): lax.all_to_all(send.reshape(devices, CAP, size, size), ('row', 'col'), sp...]
    dot_general x1 -> x0, local copies, waits for them, and re-layouts: 11.9 us -> none  [on_device(): dense = jnp.dot(selector, got_tiles, preferred_element_type=jnp.float32)]
  transfers between devices with their start and end apart: 8 -> 14, of which waited for: 5 -> 5; matrix products, arithmetic and copies ran while one was open for 16% -> 3% of each run, Pallas kernels for 0% -> 9%
where the time goes in v1:
time: 336 us; the launch traced here: 331 us
  waiting for transfers between devices  215 us (64%)
  Pallas kernels  58.1 us (17%)
  starting transfers between devices  27.8 us (8%)
  blocking collectives  16.9 us (5%)
  local copies, waits for them, and re-layouts  6.88 us (2%)
  other arithmetic  6.14 us (2%)
    ppermute x13, waiting for transfers between devices, permuted(): return lax.ppermute(value, axis, pairs)  120 us
    all_to_all x1, waiting for transfers between devices, on_device(): lax.all_to_all(send.reshape(devices, CAP, size, size), ('row', 'col'), sp...  95.7 us
    pallas_call x3, Pallas kernels, product(): pl.pallas_call(body, grid=(rows // tall,), out_shape=jax.ShapeDtypeStruct...  42.9 us
    ppermute x13, starting transfers between devices, permuted(): return lax.ppermute(value, axis, pairs)  19.2 us
    all_to_all x1, blocking collectives, on_device(): lax.all_to_all(places.reshape(devices, CAP), ('row', 'col'), split_axis=0...  16.9 us
    pallas_call x1, Pallas kernels, add_tiles(): pl.pallas_call(functools.partial(add_kernel, groups), out_shape=jax.Shape...  9.46 us
    all_to_all x1, starting transfers between devices, on_device(): lax.all_to_all(send.reshape(devices, CAP, size, size), ('row', 'col'), sp...  8.52 us
  transfers between devices with their start and end apart: 14, of which 5 were waited for; matrix products, arithmetic and copies ran while one was open for 3% of the time, Pallas kernels for 9%

profile of v1, /device:TPU:30, one launch (start us, length us, event | category | flops | bytes accessed | tf_op | source)
XLA Modules:
  0.0 331.3 jit_solution(5604812130342437602)
XLA Ops:
  0.0 5.7 %pack.1 = (bf16[256,128,128]{2,1,0:T(8,128)(2,1)}, s32[256]{0:T(256)}) custom-call(s32[128]{0:T(128)} %bitcast.6, s32[128]{0:T(128)} %place_ref.1, bf16[128,128,128]{2,1,0:T(8,128)(2,1)} %tiles_ref.1), custom_call_target="tpu_custom_call" | custom-call | tf_op jit(solution)/shard_map/pack/pallas_call | solution.py:57
  5.7 0.8 all_to_all.9
  6.5 16.9 %all_to_all.14 = s32[128,1,2]{2,1,0:T(1,128)S(1)} all-to-all(s32[128,1,2]{2,1,0:T(1,128)S(1)} %bitcast.5), channel_id=1, replica_groups=mesh['row'=8,'col'=16] {'row','col'}, dimensions={0} | all-to-all | bytes 2048 | tf_op jit(solution)/shard_map/all_to_all | solution.py:186
  23.4 8.5 %all-to-all-start.1 = ((bf16[128,2,128,128]{3,2,1,0:T(8,128)(2,1)}), bf16[128,2,128,128]{3,2,1,0:T(8,128)(2,1)}, u32[]{:S(2)}, u32[]{:S(2)}) async-start(bf16[128,2,128,128]{3,2,1,0:T(8,128)(2,1)} %bitcast.4), calls=%async_computation.1 | async-start | bytes 16777216 | tf_op jit(solution)/shard_map/all_to_all | solution.py:185
  31.9 0.5 broadcast.4
  32.4 0.7 reduce.3
  33.1 0.7 reshape.14.place_ref
  33.8 95.7 %all-to-all-done.1 = bf16[128,2,128,128]{3,2,1,0:T(8,128)(2,1)} async-done(((bf16[128,2,128,128]{3,2,1,0:T(8,128)(2,1)}), bf16[128,2,128,128]{3,2,1,0:T(8,128)(2,1)}, u32[]{:S(2)}, u32[]{:S(2)}) %all-to-all-start.1) | async-done | bytes 8388640 | tf_op jit(solution)/shard_map/all_to_all | solution.py:185
  129.5 9.5 %add_tiles.1 = bf16[3072,512]{1,0:T(8,128)(2,1)} custom-call(s32[256]{0:T(256)} %reshape.14.place_ref, bf16[256,128,128]{2,1,0:T(8,128)(2,1)} %bitcast.3.got_ref), custom_call_target="tpu_custom_call" | custom-call | tf_op jit(solution)/shard_map/add_tiles/pallas_call | solution.py:124
  139.0 1.3 slice.24.refs_1_
  140.3 0.0 copy-start.6
  140.3 0.3 collective-permute-start.11
  140.6 7.2 %collective-permute-start.3 = (bf16[512,2048]{1,0:T(8,128)(2,1)}, bf16[512,2048]{1,0:T(8,128)(2,1)S(1)}, u32[]{:S(2)}, u32[]{:S(2)}) collective-permute-start(bf16[512,2048]{1,0:T(8,128)(2,1)} %refs_4_.5), channel_id=1, source_target_pairs={{0,15},{1,0},{2,1},{3,2},{4,3},{5,4},{6,5},{7,6},{8,7},{9,8},{10,9... | collective-permute-start | bytes 6291464 | tf_op jit(solution)/shard_map/ppermute | solution.py:17
  147.8 0.2 collective-permute-start.5
  148.1 17.0 %collective-permute-done.11.refs_3_ = bf16[1024,512]{1,0:T(8,128)(2,1)} collective-permute-done((bf16[1024,512]{1,0:T(8,128)(2,1)S(1)}, bf16[1024,512]{1,0:T(8,128)(2,1)}, u32[]{:S(2)}, u32[]{:S(2)}) %collective-permute-start.11) | collective-permute-done | bytes 1048608 | tf_op jit(solution)/shard_map/ppermute | solution.py:17
  165.0 3.8 %broadcast_select_fusion = (bf16[1024,512]{1,0:T(8,128)(2,1)S(1)}, bf16[1024,512]{1,0:T(8,128)(2,1)}, bf16[1024,512]{1,0:T(8,128)(2,1)}) fusion(bf16[1024,512]{1,0:T(8,128)(2,1)} %collective-permute-done.11.refs_3_, pred[]{:T(512)S(6)} %eq.5, bf16[3072,512]{1,0:T(8,128)(2,1)} %add_tiles.1), kind=kLoop, calls=%fused_computation | loop fusion | flops 524288 | bytes 7340033 | tf_op jit(solution)/shard_map/jit(_where)/select_n | solution.py:203
  168.8 1.6 collective-permute-start.1
  170.4 0.1 collective-permute-start.8
  170.5 47.6 %collective-permute-done.3.refs_5_ = bf16[512,2048]{1,0:T(8,128)(2,1)S(1)} collective-permute-done((bf16[512,2048]{1,0:T(8,128)(2,1)}, bf16[512,2048]{1,0:T(8,128)(2,1)S(1)}, u32[]{:S(2)}, u32[]{:S(2)}) %collective-permute-start.3) | collective-permute-done | bytes 2097184 | tf_op jit(solution)/shard_map/ppermute | solution.py:17
  218.1 0.1 slice.21
  218.1 0.1 collective-permute-start.4
  218.2 39.5 %collective-permute-done.5.refs_7_ = bf16[512,2048]{1,0:T(8,128)(2,1)} collective-permute-done((bf16[512,2048]{1,0:T(8,128)(2,1)}, bf16[512,2048]{1,0:T(8,128)(2,1)}, u32[]{:S(2)}, u32[]{:S(2)}) %collective-permute-start.5) | collective-permute-done | bytes 2097184 | tf_op jit(solution)/shard_map/ppermute | solution.py:17
  257.8 1.3 slice.22
  259.1 0.1 collective-permute-start.6
  259.2 0.0 collective-permute-start.10
  259.2 0.0 collective-permute-done.1.refs_3_
  259.2 2.0 collective-permute-start.12
  261.2 0.0 collective-permute-done.8.refs_3_
  261.2 0.0 collective-permute-start.7
  261.3 1.7 broadcast_select_fusion.1
  262.9 0.0 collective-permute-done.4
  262.9 0.4 collective-permute-start.9
  263.3 0.1 constant_dynamic-update-slice_fusion.1
  263.4 15.4 %collective-permute-done.6 = bf16[512,1024]{1,0:T(8,128)(2,1)S(1)} collective-permute-done((bf16[512,1024]{1,0:T(8,128)(2,1)S(1)}, bf16[512,1024]{1,0:T(8,128)(2,1)S(1)}, u32[]{:S(2)}, u32[]{:S(2)}) %collective-permute-start.6) | collective-permute-done | bytes 1048608 | tf_op jit(solution)/shard_map/ppermute | solution.py:17
  278.9 0.1 constant_dynamic-update-slice_fusion.refs_6_
  279.0 0.0 collective-permute-start
  279.0 0.0 collective-permute-done.10.refs_0_
  279.0 1.0 copy-done.8
  280.0 7.2 %collective-permute-start.2 = (bf16[1024,512]{1,0:T(8,128)(2,1)}, bf16[1024,512]{1,0:T(8,128)(2,1)}, u32[]{:S(2)}, u32[]{:S(2)}) collective-permute-start(bf16[1024,512]{1,0:T(8,128)(2,1)} %get-tuple-element.13), channel_id=1, source_target_pairs={{0,16},{16,0},{32,48},{48,32},{64,80},{80,64},{96,112},{112,96},{1... | collective-permute-start | bytes 3145736 | tf_op jit(solution)/shard_map/ppermute | solution.py:17
  287.3 0.0 collective-permute-done.12.refs_2_
  287.3 14.3 %product.3.refs_8_ = bf16[3072,2048]{1,0:T(8,128)(2,1)} custom-call(bf16[1024,512]{1,0:T(8,128)(2,1)} %copy-done.8, bf16[1024,512]{1,0:T(8,128)(2,1)} %copy-done.6, bf16[1024,512]{1,0:T(8,128)(2,1)} %collective-permute-done.12.refs_2_, bf16[1024,512]{1,0:T(8,128)(2,1)} %collective-permute-done.11.refs_3_, bf16[512,2048]{1,0:T(8,128)(2,1)} %refs_4_.5, ...), custom_call_target="tpu_custom_call" | custom-call | flops 8589934592 | bytes 16777216 | tf_op jit(solution)/shard_map/product/pallas_call | solution.py:163
  301.5 0.0 collective-permute-done.7.refs_0_
  301.6 0.0 collective-permute-done.9.refs_2_
  301.6 14.3 %product.4.refs_8_ = bf16[3072,2048]{1,0:T(8,128)(2,1)} custom-call(bf16[1024,512]{1,0:T(8,128)(2,1)} %collective-permute-done.7.refs_0_, bf16[1024,512]{1,0:T(8,128)(2,1)} %get-tuple-element.10.refs_1_, bf16[1024,512]{1,0:T(8,128)(2,1)} %collective-permute-done.9.refs_2_, bf16[1024,512]{1,0:T(8,128)(2,1)} %copy-done.4, ...), custom_call_target="tpu_custom_call", output_to_operand_aliasing={{}: (8, {})} | custom-call | flops 8589934592 | bytes 16777216 | tf_op jit(solution)/shard_map/product/pallas_call | solution.py:163
  315.9 0.0 collective-permute-done.refs_0_
  315.9 0.0 collective-permute-done.2.refs_2_
  315.9 1.0 copy-done.5
  316.9 14.3 %product.5 = bf16[3072,2048]{1,0:T(8,128)(2,1)} custom-call(bf16[1024,512]{1,0:T(8,128)(2,1)} %copy-done.5, bf16[1024,512]{1,0:T(8,128)(2,1)} %get-tuple-element.11.refs_1_, bf16[1024,512]{1,0:T(8,128)(2,1)} %collective-permute-done.2.refs_2_, bf16[1024,512]{1,0:T(8,128)(2,1)} %copy-done.3, ...), custom_call_target="tpu_custom_call", output_to_operand_aliasing={{}: (8, {})} | custom-call | flops 8589934592 | bytes 16777216 | tf_op jit(solution)/shard_map/product/pallas_call | solution.py:163
  (15 shorter events, 0.0 us)
Async XLA Ops:
  23.4 106.1 %all-to-all-start.1 = ((bf16[128,2,128,128]{3,2,1,0:T(8,128)(2,1)}), bf16[128,2,128,128]{3,2,1,0:T(8,128)(2,1)}, u32[]{:S(2)}, u32[]{:S(2)}) async-start(bf16[128,2,128,128]{3,2,1,0:T(8,128)(2,1)} %bitcast.4), calls=%async_computation.1 | async-start | bytes 16777216 | tf_op jit(solution)/shard_map/all_to_all | solution.py:185
  140.3 28.5 %copy-start.6 = (bf16[1024,512]{1,0:T(8,128)(2,1)}, bf16[1024,512]{1,0:T(8,128)(2,1)S(1)}, u32[]{:S(2)}) copy-start(bf16[1024,512]{1,0:T(8,128)(2,1)S(1)} %slice.24.refs_1_) | copy-start | bytes 3145732
  140.3 24.7 %collective-permute-start.11 = (bf16[1024,512]{1,0:T(8,128)(2,1)S(1)}, bf16[1024,512]{1,0:T(8,128)(2,1)}, u32[]{:S(2)}, u32[]{:S(2)}) collective-permute-start(bf16[1024,512]{1,0:T(8,128)(2,1)S(1)} %slice.24.refs_1_), channel_id=1, source_target_pairs={{0,96},{16,112},{32,0},{48,16},{64,32},{80,48},{96,64},{112,80},{1... | collective-permute-start | bytes 3145736 | tf_op jit(solution)/shard_map/ppermute | solution.py:17
  140.6 77.5 %collective-permute-start.3 = (bf16[512,2048]{1,0:T(8,128)(2,1)}, bf16[512,2048]{1,0:T(8,128)(2,1)S(1)}, u32[]{:S(2)}, u32[]{:S(2)}) collective-permute-start(bf16[512,2048]{1,0:T(8,128)(2,1)} %refs_4_.5), channel_id=1, source_target_pairs={{0,15},{1,0},{2,1},{3,2},{4,3},{5,4},{6,5},{7,6},{8,7},{9,8},{10,9... | collective-permute-start | bytes 6291464 | tf_op jit(solution)/shard_map/ppermute | solution.py:17
  147.8 109.9 %collective-permute-start.5 = (bf16[512,2048]{1,0:T(8,128)(2,1)}, bf16[512,2048]{1,0:T(8,128)(2,1)}, u32[]{:S(2)}, u32[]{:S(2)}) collective-permute-start(bf16[512,2048]{1,0:T(8,128)(2,1)} %refs_4_.5), channel_id=1, source_target_pairs={{0,13},{1,14},{2,15},{3,0},{4,1},{5,2},{6,3},{7,4},{8,5},{9,6},{10... | collective-permute-start | bytes 6291464 | tf_op jit(solution)/shard_map/ppermute | solution.py:17
  168.8 92.5 %copy-start = (bf16[3072,512]{1,0:T(8,128)(2,1)S(1)}, bf16[3072,512]{1,0:T(8,128)(2,1)}, u32[]{:S(2)}) copy-start(bf16[3072,512]{1,0:T(8,128)(2,1)} %add_tiles.1) | copy-start | bytes 9437188
  168.8 90.4 %copy-start.7 = (bf16[1024,512]{1,0:T(8,128)(2,1)S(1)}, bf16[1024,512]{1,0:T(8,128)(2,1)}, u32[]{:S(2)}) copy-start(bf16[1024,512]{1,0:T(8,128)(2,1)} %copy-done.6) | copy-start | bytes 3145732
  168.8 90.4 %collective-permute-start.1 = (bf16[1024,512]{1,0:T(8,128)(2,1)}, bf16[1024,512]{1,0:T(8,128)(2,1)S(1)}, u32[]{:S(2)}, u32[]{:S(2)}) collective-permute-start(bf16[1024,512]{1,0:T(8,128)(2,1)} %get-tuple-element.11.refs_1_), channel_id=1, source_target_pairs={{0,96},{16,112},{32,0},{48,16},{64,32},{80,48},{96,64},{112,80},{1... | collective-permute-start | bytes 3145736 | tf_op jit(solution)/shard_map/ppermute | solution.py:17
  170.4 90.8 %collective-permute-start.8 = (bf16[1024,512]{1,0:T(8,128)(2,1)}, bf16[1024,512]{1,0:T(8,128)(2,1)S(1)}, u32[]{:S(2)}, u32[]{:S(2)}) collective-permute-start(bf16[1024,512]{1,0:T(8,128)(2,1)} %get-tuple-element.10.refs_1_), channel_id=1, source_target_pairs={{0,96},{16,112},{32,0},{48,16},{64,32},{80,48},{96,64},{112,80},{1... | collective-permute-start | bytes 3145736 | tf_op jit(solution)/shard_map/ppermute | solution.py:17
  218.0 44.9 %copy-start.1 = (bf16[512,2048]{1,0:T(8,128)(2,1)}, bf16[512,2048]{1,0:T(8,128)(2,1)S(1)}, u32[]{:S(2)}) copy-start(bf16[512,2048]{1,0:T(8,128)(2,1)S(1)} %collective-permute-done.3.refs_5_) | copy-start | bytes 6291460
  218.1 44.8 %collective-permute-start.4 = (bf16[512,1024]{1,0:T(8,128)(2,1)S(1)}, bf16[512,1024]{1,0:T(8,128)(2,1)S(1)}, u32[]{:S(2)}, u32[]{:S(2)}) collective-permute-start(bf16[512,1024]{1,0:T(8,128)(2,1)S(1)} %slice.21), channel_id=1, source_target_pairs={{0,15},{1,0},{2,1},{3,2},{4,3},{5,4},{6,5},{7,6},{8,7},{9,8},{10,9... | collective-permute-start | bytes 3145736 | tf_op jit(solution)/shard_map/ppermute | solution.py:17
  259.1 19.8 %collective-permute-start.6 = (bf16[512,1024]{1,0:T(8,128)(2,1)S(1)}, bf16[512,1024]{1,0:T(8,128)(2,1)S(1)}, u32[]{:S(2)}, u32[]{:S(2)}) collective-permute-start(bf16[512,1024]{1,0:T(8,128)(2,1)S(1)} %slice.22), channel_id=1, source_target_pairs={{0,1},{1,2},{2,3},{3,4},{4,5},{5,6},{6,7},{7,8},{8,9},{9,10},{10,1... | collective-permute-start | bytes 3145736 | tf_op jit(solution)/shard_map/ppermute | solution.py:17
  259.2 19.8 %collective-permute-start.10 = (bf16[1024,512]{1,0:T(8,128)(2,1)S(1)}, bf16[1024,512]{1,0:T(8,128)(2,1)S(1)}, u32[]{:S(2)}, u32[]{:S(2)}) collective-permute-start(bf16[1024,512]{1,0:T(8,128)(2,1)S(1)} %copy-done.7), channel_id=1, source_target_pairs={{0,16},{16,32},{32,48},{48,64},{64,80},{80,96},{96,112},{112,0},{1... | collective-permute-start | bytes 3145736 | tf_op jit(solution)/shard_map/ppermute | solution.py:17
  259.2 3.7 %copy-start.3 = (bf16[1024,512]{1,0:T(8,128)(2,1)}, bf16[1024,512]{1,0:T(8,128)(2,1)S(1)}, u32[]{:S(2)}) copy-start(bf16[1024,512]{1,0:T(8,128)(2,1)S(1)} %collective-permute-done.1.refs_3_) | copy-start | bytes 3145732
  259.2 28.1 %collective-permute-start.12 = (bf16[1024,512]{1,0:T(8,128)(2,1)S(1)}, bf16[1024,512]{1,0:T(8,128)(2,1)}, u32[]{:S(2)}, u32[]{:S(2)}) collective-permute-start(bf16[1024,512]{1,0:T(8,128)(2,1)S(1)} %get-tuple-element.9), channel_id=1, source_target_pairs={{0,16},{16,0},{32,48},{48,32},{64,80},{80,64},{96,112},{112,96},{1... | collective-permute-start | bytes 3145736 | tf_op jit(solution)/shard_map/ppermute | solution.py:17
  261.2 1.7 copy-start.4
  261.2 40.3 %collective-permute-start.7 = (bf16[1024,512]{1,0:T(8,128)(2,1)}, bf16[1024,512]{1,0:T(8,128)(2,1)}, u32[]{:S(2)}, u32[]{:S(2)}) collective-permute-start(bf16[1024,512]{1,0:T(8,128)(2,1)} %get-tuple-element.10.refs_1_), channel_id=1, source_target_pairs={{0,16},{16,32},{32,48},{48,64},{64,80},{80,96},{96,112},{112,0},{1... | collective-permute-start | bytes 3145736 | tf_op jit(solution)/shard_map/ppermute | solution.py:17
  262.9 38.6 %collective-permute-start.9 = (bf16[1024,512]{1,0:T(8,128)(2,1)}, bf16[1024,512]{1,0:T(8,128)(2,1)}, u32[]{:S(2)}, u32[]{:S(2)}) collective-permute-start(bf16[1024,512]{1,0:T(8,128)(2,1)} %get-tuple-element.12), channel_id=1, source_target_pairs={{0,16},{16,0},{32,48},{48,32},{64,80},{80,64},{96,112},{112,96},{1... | collective-permute-start | bytes 3145736 | tf_op jit(solution)/shard_map/ppermute | solution.py:17
  278.9 8.3 %copy-start.2 = (bf16[512,2048]{1,0:T(8,128)(2,1)}, bf16[512,2048]{1,0:T(8,128)(2,1)S(1)}, u32[]{:S(2)}) copy-start(bf16[512,2048]{1,0:T(8,128)(2,1)S(1)} %constant_dynamic-update-slice_fusion.refs_6_) | copy-start | bytes 6291460
  279.0 36.9 %collective-permute-start = (bf16[1024,512]{1,0:T(8,128)(2,1)}, bf16[1024,512]{1,0:T(8,128)(2,1)S(1)}, u32[]{:S(2)}, u32[]{:S(2)}) collective-permute-start(bf16[1024,512]{1,0:T(8,128)(2,1)} %get-tuple-element.11.refs_1_), channel_id=1, source_target_pairs={{0,16},{16,32},{32,48},{48,64},{64,80},{80,96},{96,112},{112,0},{1... | collective-permute-start | bytes 3145736 | tf_op jit(solution)/shard_map/ppermute | solution.py:17
  279.0 1.1 copy-start.8
  280.0 35.9 %collective-permute-start.2 = (bf16[1024,512]{1,0:T(8,128)(2,1)}, bf16[1024,512]{1,0:T(8,128)(2,1)}, u32[]{:S(2)}, u32[]{:S(2)}) collective-permute-start(bf16[1024,512]{1,0:T(8,128)(2,1)} %get-tuple-element.13), channel_id=1, source_target_pairs={{0,16},{16,0},{32,48},{48,32},{64,80},{80,64},{96,112},{112,96},{1... | collective-permute-start | bytes 3145736 | tf_op jit(solution)/shard_map/ppermute | solution.py:17
  315.9 1.0 copy-start.5
